TPU v7x, 128 devices: a whole 4x4x4 slice. The times are simulated.
128 devices in a mesh: dp: 16 (over y, x), expert: 4 (over z), tensor: 2 (over core).
Axes of the slice: x: 4, y: 4, z: 4, core: 2. Of those that a mesh axis runs over, the one named last changes fastest.
Arguments:
- tokens: bfloat16 [8192, 2048], P(('dp', 'expert')), may hold values from -6 to 6
- expert_ids: int32 [8192, 2], P(('dp', 'expert')), may hold values from 0 to 3, all different within a row; in each aligned block of 128 rows (0 to 127, 128 to 255, ...) at most 96 rows name the same one
- gate_values: float32 [8192, 2], P(('dp', 'expert')), may hold values from 0.1 to 1
- tag_labels: int32 [8192], P(('dp', 'expert')), may hold values from 0 to 31
- w_gate: bfloat16 [4, 2048, 7168], P('expert', 'dp', 'tensor'), may hold values from -0.125 to 0.125
- w_up: bfloat16 [4, 2048, 7168], P('expert', 'dp', 'tensor'), may hold values from -0.125 to 0.125
- w_down: bfloat16 [4, 7168, 2048], P('expert', 'tensor', 'dp'), may hold values from -0.0625 to 0.0625
- adapter_in: bfloat16 [4, 16, 2048], P('expert'), may hold values from -0.125 to 0.125
- adapter_out: bfloat16 [4, 16, 7168], P('expert', None, 'tensor'), may hold values from -1.5 to 1.5
- tag_weight: bfloat16 [2048, 32], replicated, may hold values from -0.125 to 0.125
Outputs:
- layer_out: bfloat16 [8192, 2048], P(('dp', 'expert'), 'tensor')
- in_gradient: float32 [4, 16, 2048], P('expert')
- out_gradient: float32 [4, 16, 7168], P('expert', None, 'tensor')
Inputs may be any that keep to these rules, and one draw needn't show every extreme that they name: `expert_ids`: each row names 2 different experts; the rows of one index of dp and expert name each expert at most 96 times, a bound that some block reaches.
All inputs are finite; a program needn't handle non-finite values.
Results may differ from a plain program's by a relative error of at most 0.017.
Values may be sent and summed in bfloat16 or wider, within the bound.
A program may use at most 128 MiB of HBM per device.

v0:
```python
import jax
import jax.numpy as jnp
from jax import lax
from jax.sharding import PartitionSpec as P

adapter_scale = 2.0


def contract_last(left, right):
    return lax.dot_general(
        left, right, (((1,), (1,)), ((), ())), preferred_element_type=jnp.float32
    )


def contract_first(left, right):
    return lax.dot_general(
        left, right, (((0,), (0,)), ((), ())), preferred_element_type=jnp.float32
    )


def tag_gradient(logits, tag_labels):
    exp_logits = jnp.exp(logits)
    probability = exp_logits / jnp.sum(exp_logits, axis=1, keepdims=True)
    labels_hot = (
        tag_labels[:, None] == jnp.arange(logits.shape[1], dtype=jnp.int32)[None, :]
    ).astype(jnp.float32)
    return probability - labels_hot


def local(
    tokens,
    expert_ids,
    gate_values,
    tag_labels,
    w_gate,
    w_up,
    w_down,
    adapter_in,
    adapter_out,
    tag_weight,
):
    experts = lax.axis_size("expert")
    shards = lax.axis_size("tensor")
    tok_count = tokens.shape[0]
    model_width = tokens.shape[1]
    share_width = model_width // shards
    capacity = 3 * tok_count // experts
    slot_count = experts * capacity
    flat_ids = expert_ids.reshape(-1)
    onehot = (flat_ids[:, None] == jnp.arange(experts, dtype=jnp.int32)[None, :]).astype(jnp.int32)
    before = jnp.cumsum(onehot, axis=0) - onehot
    position = jnp.sum(before * onehot, axis=1)
    slot_index = (flat_ids * capacity + position).reshape(tok_count, expert_ids.shape[1])
    matches = jnp.arange(slot_count, dtype=jnp.int32)[:, None, None] == slot_index[None, :, :]
    dispatch = jnp.sum(matches.astype(jnp.float32), axis=2).astype(jnp.bfloat16)
    combine = jnp.sum(jnp.where(matches, gate_values[None, :, :], jnp.float32(0.0)), axis=2).T
    outgoing = jnp.dot(dispatch, tokens, preferred_element_type=jnp.float32).astype(jnp.bfloat16)
    arrived = lax.all_to_all(
        outgoing.reshape(experts, capacity, model_width),
        "expert",
        split_axis=0,
        concat_axis=0,
        tiled=True,
    ).reshape(slot_count, model_width)
    gate_acc = jnp.dot(
        arrived,
        lax.all_gather(w_gate, "dp", axis=1, tiled=True)[0],
        preferred_element_type=jnp.float32,
    )
    up_acc = jnp.dot(
        arrived,
        lax.all_gather(w_up, "dp", axis=1, tiled=True)[0],
        preferred_element_type=jnp.float32,
    )
    low_rank = contract_last(arrived, adapter_in[0]).astype(jnp.bfloat16)
    up_full = up_acc + adapter_scale * jnp.dot(
        low_rank, adapter_out[0], preferred_element_type=jnp.float32
    )
    activated = jax.nn.silu(gate_acc)
    hidden = (activated * up_full).astype(jnp.bfloat16)
    down_full = lax.all_gather(w_down, "dp", axis=2, tiled=True)[0]
    partial_value = jnp.dot(hidden, down_full, preferred_element_type=jnp.float32)
    column_start = lax.axis_index("tensor") * share_width
    summed = lax.psum(partial_value, "tensor").astype(jnp.bfloat16)
    returned = lax.all_to_all(
        summed.reshape(experts, capacity, model_width),
        "expert",
        split_axis=0,
        concat_axis=0,
        tiled=True,
    ).reshape(slot_count, model_width)
    mixed_rows = tokens.astype(jnp.float32) + jnp.dot(
        combine, returned.astype(jnp.float32), precision=lax.Precision.HIGHEST
    )
    layer_full = mixed_rows.astype(jnp.bfloat16)
    logits = jnp.dot(layer_full, tag_weight, preferred_element_type=jnp.float32)
    logit_grad = tag_gradient(logits, tag_labels)
    upstream = jnp.dot(
        logit_grad, tag_weight.astype(jnp.float32).T, precision=lax.Precision.HIGHEST
    )
    slot_out = jnp.dot(combine.T, upstream, precision=lax.Precision.HIGHEST).astype(jnp.bfloat16)
    slot_grad = lax.all_to_all(
        slot_out.reshape(experts, capacity, model_width),
        "expert",
        split_axis=0,
        concat_axis=0,
        tiled=True,
    ).reshape(slot_count, model_width)
    layer_out = lax.dynamic_slice_in_dim(layer_full, column_start, share_width, 1)
    hidden_grad = contract_last(slot_grad, down_full)
    up_grad = (hidden_grad * activated).astype(jnp.bfloat16)
    out_local = adapter_scale * contract_first(low_rank, up_grad)
    low_grad = adapter_scale * contract_last(up_grad, adapter_out[0])
    in_local = lax.dot_general(
        low_grad,
        arrived.astype(jnp.float32),
        (((0,), (0,)), ((), ())),
        precision=lax.Precision.HIGHEST,
    )
    in_total = lax.psum(in_local.astype(jnp.bfloat16), ("dp", "tensor")).astype(jnp.float32)
    out_total = lax.psum(out_local.astype(jnp.bfloat16), "dp").astype(jnp.float32)
    return (layer_out, in_total[None], out_total[None])


def solution(mesh):
    in_specs = (
        P(("dp", "expert"), None),
        P(("dp", "expert"), None),
        P(("dp", "expert"), None),
        P(("dp", "expert")),
        P("expert", "dp", "tensor"),
        P("expert", "dp", "tensor"),
        P("expert", "tensor", "dp"),
        P("expert", None, None),
        P("expert", None, "tensor"),
        P(),
    )
    out_specs = (
        P(("dp", "expert"), "tensor"),
        P("expert", None, None),
        P("expert", None, "tensor"),
    )
    return jax.shard_map(local, mesh=mesh, in_specs=in_specs, out_specs=out_specs, check_vma=False)
```

profile of v0, /device:TPU:0, one launch (start us, length us, event | category | flops | bytes accessed | tf_op | source)
XLA Modules:
  0.0 610.8 jit_solution(16985919612496595279)
XLA Ops:
  7.2 0.0 all-gather.6.cloned.1.call-start
  7.2 0.7 all-gather.6.cloned.1.call-update
  7.9 0.0 all-gather.4.cloned.1.call-start
  8.0 0.7 all-gather.4.cloned.1.call-update
  8.7 0.0 all-gather.8.cloned.1.call-start
  8.7 0.7 all-gather.8.cloned.1.call-update
  9.4 0.8 copy.31
  10.2 0.1 eq.56
  10.4 0.1 eq.52
  10.5 1.2 reduce-window.6
  11.8 0.1 slice.8
  11.8 0.1 copy.33
  12.0 0.1 copy.34
  12.1 0.1 add_bitcast_fusion
  12.2 0.1 reduce_sum.39
  12.3 0.1 copy.35
  12.4 0.7 multiply_add_fusion
  13.1 0.8 convert_reduce_fusion
  13.9 0.6 convolution_convert_fusion.1
  14.4 25.9 %all_to_all.15 = bf16[4,96,2048]{2,1,0:T(8,128)(2,1)S(1)} all-to-all(bf16[4,96,2048]{2,1,0:T(8,128)(2,1)S(1)} %bitcast.78), channel_id=1, replica_groups=mesh['dp'=16,'expert'=4,'tensor'=2] {'expert'}, dimensions={0} | all-to-all | bytes 3145728 | tf_op jit(solution)/shard_map/all_to_all | solution.py:58
  40.4 0.5 convolution_convert_fusion.3
  40.9 72.1 %all-gather.6.cloned.1.call-done = bf16[1,2048,3584]{2,1,0:T(8,128)(2,1)} async-done(((bf16[1,128,3584]{2,1,0:T(8,128)(2,1)}), bf16[1,2048,3584]{2,1,0:T(8,128)(2,1)}) %all-gather.6.cloned.1.call-update) | async-done | bytes 14680080 | tf_op jit(solution)/shard_map/all_gather | solution.py:72
  113.0 11.5 %fusion.4 = f32[384,3584]{1,0:T(8,128)} fusion(bf16[384,2048]{1,0:T(8,128)(2,1)S(1)} %bitcast.75, bf16[1,2048,3584]{2,1,0:T(8,128)(2,1)} %all-gather.6.cloned.1.call-done), kind=kOutput, calls=%fused_computation.4 | convolution fusion | flops 5637144576 | bytes 21757952 | tf_op jit(solution)/shard_map/dot_general | solution.py:70
  124.5 90.7 %all-gather.4.cloned.1.call-done = bf16[1,2048,3584]{2,1,0:T(8,128)(2,1)} async-done(((bf16[1,128,3584]{2,1,0:T(8,128)(2,1)}), bf16[1,2048,3584]{2,1,0:T(8,128)(2,1)}) %all-gather.4.cloned.1.call-update) | async-done | bytes 14680080 | tf_op jit(solution)/shard_map/all_gather | solution.py:67
  215.2 11.1 %divide_multiply_fusion = f32[384,3584]{1,0:T(8,128)} fusion(bf16[384,2048]{1,0:T(8,128)(2,1)S(1)} %bitcast.76, bf16[1,2048,3584]{2,1,0:T(8,128)(2,1)} %all-gather.4.cloned.1.call-done), kind=kOutput, calls=%fused_computation.14 | convolution fusion | flops 5642649600 | bytes 21757952 | tf_op jit(solution)/shard_map/dot_general | solution.py:65
  226.4 99.8 %all-gather.8.cloned.1.call-done = bf16[1,3584,2048]{2,1,0:T(8,128)(2,1)} async-done(((bf16[1,3584,128]{2,1,0:T(8,128)(2,1)}), bf16[1,3584,2048]{2,1,0:T(8,128)(2,1)}) %all-gather.8.cloned.1.call-update) | async-done | bytes 14680080 | tf_op jit(solution)/shard_map/all_gather | solution.py:81
  326.1 15.2 %fusion.2 = f32[384,2048]{1,0:T(8,128)} fusion(bf16[1,3584,2048]{2,1,0:T(8,128)(2,1)} %all-gather.8.cloned.1.call-done, f32[384,3584]{1,0:T(8,128)} %divide_multiply_fusion, f32[384,3584]{1,0:T(8,128)} %fusion.4, bf16[384,16]{0,1:T(8,128)(2,1)S(1)} %convolution_convert_fusion.3, bf16[1,16,3584]{2,1,0:T(8,128)(2,1)S(1)} %copy-done.4), kind=kOutput, calls=%fused_computation.2 | convolution fusion | flops 5686689792 | bytes 28962816 | tf_op jit(solution)/shard_map/dot_general | solution.py:82
  341.3 12.2 %all-reduce.7 = bf16[384,2048]{1,0:T(8,128)(2,1)S(1)} all-reduce(f32[384,2048]{1,0:T(8,128)} %fusion.2), channel_id=1, replica_groups=mesh['dp'=16,'expert'=4,'tensor'=2] {'tensor'}, use_global_device_ids=true, to_apply=%region_5.6 | all-reduce | flops 786432 | bytes 4718592 | tf_op jit(solution)/shard_map/psum | solution.py:84
  353.6 25.5 %all_to_all.16 = bf16[4,96,2048]{2,1,0:T(8,128)(2,1)S(1)} all-to-all(bf16[4,96,2048]{2,1,0:T(8,128)(2,1)S(1)} %bitcast.80), channel_id=1, replica_groups=mesh['dp'=16,'expert'=4,'tensor'=2] {'expert'}, dimensions={0} | all-to-all | bytes 3145728 | tf_op jit(solution)/shard_map/all_to_all | solution.py:85
  379.0 1.0 fusion.21
  380.1 0.3 fusion.38
  380.4 0.6 fusion.28
  381.0 3.7 convolution_convert_fusion
  384.8 4.4 all-to-all-start.2
  389.1 0.0 all-reduce.4.cloned.1.call-start
  389.2 20.4 %all-to-all-done.2 = bf16[4,96,2048]{2,1,0:T(8,128)(2,1)} async-done(((bf16[4,96,2048]{2,1,0:T(8,128)(2,1)}), bf16[4,96,2048]{2,1,0:T(8,128)(2,1)}, u32[]{:S(2)}, u32[]{:S(2)}) %all-to-all-start.2) | async-done | bytes 1572896 | tf_op jit(solution)/shard_map/all_to_all | solution.py:102
  409.6 10.4 %fusion.13 = bf16[384,3584]{1,0:T(8,128)(2,1)S(1)} fusion(f32[384,3584]{1,0:T(8,128)} %divide_multiply_fusion, bf16[384,2048]{1,0:T(8,128)(2,1)} %bitcast.12, bf16[1,3584,2048]{2,1,0:T(8,128)(2,1)} %all-gather.8.cloned.1.call-done), kind=kOutput, calls=%fused_computation.12 | convolution fusion | flops 5639897088 | bytes 24510464 | tf_op jit(solution)/shard_map/dot_general | solution.py:10
  420.0 0.8 convolution_multiply_fusion.2
  420.9 0.6 copy-done.2
  421.4 1.4 fusion.22
  422.8 0.0 all-reduce.4.cloned.1.call-update
  422.8 0.0 all-reduce.6.cloned.1.call-start
  422.9 1.1 fusion.20
  424.0 0.7 constant_dynamic-slice_fusion
  424.7 92.3 %all-reduce.4.cloned.1.call-done = bf16[1,16,2048]{2,1,0:T(8,128)(2,1)} async-done(((bf16[1,16,2048]{2,1,0:T(8,128)(2,1)}), bf16[1,16,2048]{2,1,0:T(8,128)(2,1)}) %all-reduce.4.cloned.1.call-update) | async-done | bytes 65552 | tf_op jit(solution)/shard_map/psum | solution.py:120
  517.0 1.5 broadcast_in_dim.33
  518.5 84.1 %all-reduce.6.cloned.1.call-done = bf16[1,16,3584]{2,1,0:T(8,128)(2,1)} async-done(((bf16[1,16,3584]{2,1,0:T(8,128)(2,1)}), bf16[1,16,3584]{2,1,0:T(8,128)(2,1)}) %all-reduce.6.cloned.1.call-update) | async-done | bytes 114704 | tf_op jit(solution)/shard_map/psum | solution.py:121
  602.7 1.6 broadcast_in_dim.35
  (18 shorter events, 0.1 us)
Async XLA Ops:
  7.2 372.9 %copy-start = (bf16[2048,32]{0,1:T(8,128)(2,1)S(1)}, bf16[2048,32]{0,1:T(8,128)(2,1)}, u32[]{:S(2)}) copy-start(bf16[2048,32]{0,1:T(8,128)(2,1)} %param.19) | copy-start | bytes 393220
  7.2 6.7 %copy-start.3 = (bf16[128,2048]{1,0:T(8,128)(2,1)S(1)}, bf16[128,2048]{1,0:T(8,128)(2,1)}, u32[]{:S(2)}) copy-start(bf16[128,2048]{1,0:T(8,128)(2,1)} %param.10) | copy-start | bytes 1572868
  7.2 105.8 %all-gather.6.cloned.1.call-start = ((), (), s32[]{:S(2)}) async-start(), calls=%async_computation.4 | async-start | bytes 15597568 | tf_op jit(solution)/shard_map/all_gather | solution.py:72
  7.9 207.3 %all-gather.4.cloned.1.call-start = ((), (), s32[]{:S(2)}) async-start(), calls=%async_computation.3 | async-start | bytes 15597568 | tf_op jit(solution)/shard_map/all_gather | solution.py:67
  8.7 317.4 %all-gather.8.cloned.1.call-start = ((), (), s32[]{:S(2)}) async-start(), calls=%async_computation.5 | async-start | bytes 15597568 | tf_op jit(solution)/shard_map/all_gather | solution.py:81
  9.4 31.0 %copy-start.5 = (bf16[1,16,2048]{2,1,0:T(8,128)(2,1)S(1)}, bf16[1,16,2048]{2,1,0:T(8,128)(2,1)}, u32[]{:S(2)}) copy-start(bf16[1,16,2048]{2,1,0:T(8,128)(2,1)} %param.17) | copy-start | bytes 196612
  40.4 174.9 %copy-start.1 = (bf16[4,96,2048]{2,1,0:T(8,128)(2,1)}, bf16[4,96,2048]{2,1,0:T(8,128)(2,1)S(1)}, u32[]{:S(2)}) copy-start(bf16[4,96,2048]{2,1,0:T(8,128)(2,1)S(1)} %all_to_all.15) | copy-start | bytes 4718596
  124.5 201.6 %copy-start.4 = (bf16[1,16,3584]{2,1,0:T(8,128)(2,1)S(1)}, bf16[1,16,3584]{2,1,0:T(8,128)(2,1)}, u32[]{:S(2)}) copy-start(bf16[1,16,3584]{2,1,0:T(8,128)(2,1)} %param.18) | copy-start | bytes 344068
  353.6 26.8 %copy-start.6 = (s32[128]{0:T(128)S(1)}, s32[128]{0:T(128)}, u32[]{:S(2)}) copy-start(s32[128]{0:T(128)} %param.13) | copy-start | bytes 1540
  384.8 24.8 %all-to-all-start.2 = ((bf16[4,96,2048]{2,1,0:T(8,128)(2,1)}), bf16[4,96,2048]{2,1,0:T(8,128)(2,1)}, u32[]{:S(2)}, u32[]{:S(2)}) async-start(bf16[4,96,2048]{2,1,0:T(8,128)(2,1)} %bitcast.11), calls=%async_computation.2 | async-start | bytes 3145728 | tf_op jit(solution)/shard_map/all_to_all | solution.py:102
  389.1 127.9 %all-reduce.4.cloned.1.call-start = ((), (), s32[]{:S(2)}) async-start(), calls=%async_computation.6 | async-start | bytes 131072 | tf_op jit(solution)/shard_map/psum | solution.py:120
  420.0 1.4 copy-start.2
  422.8 179.9 %all-reduce.6.cloned.1.call-start = ((), (), s32[]{:S(2)}) async-start(), calls=%async_computation.7 | async-start | bytes 229376 | tf_op jit(solution)/shard_map/psum | solution.py:121
Sparse Core Ops, SparseCore 0:
  10.1 102.8 all-gather.5
  115.2 100.0 all-gather.3
  217.4 108.6 all-gather.7
  422.9 94.0 all-reduce.3
  520.7 81.9 all-reduce.5
where the time goes:
time: 611 us
  waiting for transfers between devices  462 us (76%)
  blocking collectives  63.6 us (10%)
  matrix products  58.3 us (10%)
  between operations  13.9 us (2%)
    all_gather x1, waiting for transfers between devices, local(): down_full = lax.all_gather(w_down, 'dp', axis=2, tiled=True)[0]  99.8 us
    psum x1, waiting for transfers between devices, local(): lax.psum(in_local.astype(jnp.bfloat16), ('dp', 'tensor'))  92.3 us
    all_gather x1, waiting for transfers between devices, local(): lax.all_gather(w_gate, 'dp', axis=1, tiled=True)[0]  90.7 us
    psum x1, waiting for transfers between devices, local(): lax.psum(out_local.astype(jnp.bfloat16), 'dp').astype(jnp.float32)  84.1 us
    all_gather x1, waiting for transfers between devices, local(): lax.all_gather(w_up, 'dp', axis=1, tiled=True)[0]  72.1 us
    all_to_all x1, blocking collectives, local(): lax.all_to_all(outgoing.reshape(experts, capacity, model_width), 'expert'...  25.9 us
    all_to_all x1, blocking collectives, local(): lax.all_to_all(summed.reshape(experts, capacity, model_width), 'expert',...  25.5 us
    all_to_all x1, waiting for transfers between devices, local(): lax.all_to_all(slot_out.reshape(experts, capacity, model_width), 'expert'...  20.4 us
  transfers between devices with their start and end apart: 6, of which 6 were waited for; matrix products, arithmetic and copies ran while one was open for 5% of the time, Pallas kernels for 0%

commit v1 on v0

--- a/solution.py
+++ b/solution.py
@@ -4,6 +4,12 @@
 from jax.sharding import PartitionSpec as P
 
 adapter_scale = 2.0
+lines_unite = lambda in_array, mesh_name: jnp.concatenate(
+    lax.all_to_all(
+        jnp.stack(lax.psum(1, mesh_name) * [in_array], 0), mesh_name, split_axis=0, concat_axis=0
+    ),
+    1,
+)
 
 
 def contract_last(left, right):
@@ -67,11 +73,7 @@
         lax.all_gather(w_gate, "dp", axis=1, tiled=True)[0],
         preferred_element_type=jnp.float32,
     )
-    up_acc = jnp.dot(
-        arrived,
-        lax.all_gather(w_up, "dp", axis=1, tiled=True)[0],
-        preferred_element_type=jnp.float32,
-    )
+    up_acc = jnp.dot(arrived, lines_unite(w_up, "dp")[0], preferred_element_type=jnp.float32)
     low_rank = contract_last(arrived, adapter_in[0]).astype(jnp.bfloat16)
     up_full = up_acc + adapter_scale * jnp.dot(
         low_rank, adapter_out[0], preferred_element_type=jnp.float32

time: 611 us -> 685 us (1.12)
  waiting for transfers between devices: 462 us -> 520 us
  local copies, waits for them, and re-layouts: 2.94 us -> 10.6 us
    all_to_all x0 -> x1, waiting for transfers between devices: none -> 249 us  [lax.all_to_all(jnp.stack(lax.psum(1, mesh_name) * [in_array], 0), mesh_na...]
    all_gather x1, waiting for transfers between devices: 90.7 us -> 0.01 us  [local(): lax.all_gather(w_gate, 'dp', axis=1, tiled=True)[0]]
    all_gather x1 -> x0, waiting for transfers between devices: 72.1 us -> none  [local(): lax.all_gather(w_up, 'dp', axis=1, tiled=True)[0]]
    all_gather x1, waiting for transfers between devices: 99.8 us -> 72.2 us  [local(): down_full = lax.all_gather(w_down, 'dp', axis=2, tiled=True)[0]]
    all_to_all x0 -> x1, starting transfers between devices: none -> 7.21 us  [lax.all_to_all(jnp.stack(lax.psum(1, mesh_name) * [in_array], 0), mesh_na...]
  transfers between devices with their start and end apart: 6 -> 6, of which waited for: 6 -> 5; matrix products, arithmetic and copies ran while one was open for 5% -> 6% of each run, Pallas kernels for 0% -> 0%
where the time goes in v1:
time: 685 us; the launch traced here: 684 us
  waiting for transfers between devices  520 us (76%)
  blocking collectives  63.8 us (9%)
  matrix products  59.4 us (9%)
  between operations  13.9 us (2%)
  starting transfers between devices  10.9 us (2%)
  local copies, waits for them, and re-layouts  10.6 us (2%)
    all_to_all x1, waiting for transfers between devices, lax.all_to_all(jnp.stack(lax.psum(1, mesh_name) * [in_array], 0), mesh_na...  249 us
    psum x1, waiting for transfers between devices, local(): lax.psum(in_local.astype(jnp.bfloat16), ('dp', 'tensor'))  92.3 us
    psum x1, waiting for transfers between devices, local(): lax.psum(out_local.astype(jnp.bfloat16), 'dp').astype(jnp.float32)  84.2 us
    all_gather x1, waiting for transfers between devices, local(): down_full = lax.all_gather(w_down, 'dp', axis=2, tiled=True)[0]  72.2 us
    all_to_all x1, blocking collectives, local(): lax.all_to_all(outgoing.reshape(experts, capacity, model_width), 'expert'...  25.9 us
    all_to_all x1, blocking collectives, local(): lax.all_to_all(summed.reshape(experts, capacity, model_width), 'expert',...  25.5 us
    all_to_all x1, waiting for transfers between devices, local(): lax.all_to_all(slot_out.reshape(experts, capacity, model_width), 'expert'...  20.3 us
    dot_general x1, matrix products, local(): jnp.dot(hidden, down_full, preferred_element_type=jnp.float32)  15.2 us
  transfers between devices with their start and end apart: 6, of which 5 were waited for; matrix products, arithmetic and copies ran while one was open for 6% of the time, Pallas kernels for 0%

profile of v1, /device:TPU:0, one launch (start us, length us, event | category | flops | bytes accessed | tf_op | source)
XLA Modules:
  0.0 684.2 jit_solution(16133766996469841863)
XLA Ops:
  7.2 0.0 all-gather.3.cloned.1.call-start
  7.2 0.7 all-gather.3.cloned.1.call-update
  7.9 0.0 all-gather.5.cloned.1.call-start
  8.0 0.7 all-gather.5.cloned.1.call-update
  8.7 0.9 copy.31
  9.5 0.1 eq.56
  9.7 0.1 eq.52
  9.8 1.2 reduce-window.6
  11.1 0.1 slice.8
  11.1 0.1 copy.33
  11.3 0.1 copy.34
  11.4 0.1 add_bitcast_fusion
  11.5 0.1 reduce_sum.39
  11.6 0.1 copy.35
  11.7 0.7 multiply_add_fusion
  12.4 0.8 convert_reduce_fusion
  13.2 1.6 convolution_convert_fusion.1
  14.8 25.9 %all_to_all.20 = bf16[4,96,2048]{2,1,0:T(8,128)(2,1)S(1)} all-to-all(bf16[4,96,2048]{2,1,0:T(8,128)(2,1)S(1)} %bitcast.78), channel_id=1, replica_groups=mesh['dp'=16,'expert'=4,'tensor'=2] {'expert'}, dimensions={0} | all-to-all | bytes 3145728 | tf_op jit(solution)/shard_map/all_to_all | solution.py:64
  40.7 6.5 stack.2
  47.2 7.2 %all-to-all-start.1 = ((bf16[16,1,128,3584]{3,2,1,0:T(8,128)(2,1)}), bf16[16,1,128,3584]{3,2,1,0:T(8,128)(2,1)}, u32[]{:S(2)}, u32[]{:S(2)}) async-start(bf16[16,1,128,3584]{3,2,1,0:T(8,128)(2,1)} %stack.2), calls=%async_computation.1 | async-start | bytes 29360128 | tf_op jit(solution)/shard_map/all_to_all | solution.py:8
  54.5 0.5 convolution_convert_fusion.3
  55.0 249.1 %all-to-all-done.1 = bf16[16,1,128,3584]{3,2,1,0:T(8,128)(2,1)} async-done(((bf16[16,1,128,3584]{3,2,1,0:T(8,128)(2,1)}), bf16[16,1,128,3584]{3,2,1,0:T(8,128)(2,1)}, u32[]{:S(2)}, u32[]{:S(2)}) %all-to-all-start.1) | async-done | bytes 14680096 | tf_op jit(solution)/shard_map/all_to_all | solution.py:8
  304.1 11.5 %fusion.37 = f32[384,3584]{1,0:T(8,128)} fusion(bf16[384,2048]{1,0:T(8,128)(2,1)S(1)} %bitcast.75, bf16[2048,3584]{1,0:T(8,128)(2,1)} %bitcast.6), kind=kOutput, calls=%fused_computation.50 | convolution fusion | flops 5637144576 | bytes 21757952 | tf_op jit(solution)/shard_map/dot_general | solution.py:76
  315.6 11.2 %divide_multiply_fusion = f32[384,3584]{1,0:T(8,128)} fusion(bf16[384,2048]{1,0:T(8,128)(2,1)S(1)} %bitcast.76, bf16[1,2048,3584]{2,1,0:T(8,128)(2,1)} %all-gather.3.cloned.1.call-done), kind=kOutput, calls=%fused_computation.12 | convolution fusion | flops 5642649600 | bytes 21757952 | tf_op jit(solution)/shard_map/dot_general | solution.py:71
  326.8 72.2 %all-gather.5.cloned.1.call-done = bf16[1,3584,2048]{2,1,0:T(8,128)(2,1)} async-done(((bf16[1,3584,128]{2,1,0:T(8,128)(2,1)}), bf16[1,3584,2048]{2,1,0:T(8,128)(2,1)}) %all-gather.5.cloned.1.call-update) | async-done | bytes 14680080 | tf_op jit(solution)/shard_map/all_gather | solution.py:83
  399.0 15.2 %fusion.2 = f32[384,2048]{1,0:T(8,128)} fusion(bf16[1,3584,2048]{2,1,0:T(8,128)(2,1)} %all-gather.5.cloned.1.call-done, f32[384,3584]{1,0:T(8,128)} %divide_multiply_fusion, f32[384,3584]{1,0:T(8,128)} %fusion.37, bf16[384,16]{0,1:T(8,128)(2,1)S(1)} %convolution_convert_fusion.3, bf16[1,16,3584]{2,1,0:T(8,128)(2,1)S(1)} %copy-done.6), kind=kOutput, calls=%fused_computation.2 | convolution fusion | flops 5686689792 | bytes 28962816 | tf_op jit(solution)/shard_map/dot_general | solution.py:84
  414.1 12.4 %all-reduce.7 = bf16[384,2048]{1,0:T(8,128)(2,1)S(1)} all-reduce(f32[384,2048]{1,0:T(8,128)} %fusion.2), channel_id=1, replica_groups=mesh['dp'=16,'expert'=4,'tensor'=2] {'tensor'}, use_global_device_ids=true, to_apply=%region_5.6 | all-reduce | flops 786432 | bytes 4718592 | tf_op jit(solution)/shard_map/psum | solution.py:86
  426.5 25.5 %all_to_all.21 = bf16[4,96,2048]{2,1,0:T(8,128)(2,1)S(1)} all-to-all(bf16[4,96,2048]{2,1,0:T(8,128)(2,1)S(1)} %bitcast.80), channel_id=1, replica_groups=mesh['dp'=16,'expert'=4,'tensor'=2] {'expert'}, dimensions={0} | all-to-all | bytes 3145728 | tf_op jit(solution)/shard_map/all_to_all | solution.py:87
  452.0 1.0 fusion.19
  453.1 0.3 fusion.36
  453.4 0.6 fusion.26
  454.0 3.8 convolution_convert_fusion
  457.8 3.6 all-to-all-start.3
  461.4 0.0 all-reduce.4.cloned.1.call-start
  461.4 20.3 %all-to-all-done.3 = bf16[4,96,2048]{2,1,0:T(8,128)(2,1)S(1)} async-done(((bf16[4,96,2048]{2,1,0:T(8,128)(2,1)}), bf16[4,96,2048]{2,1,0:T(8,128)(2,1)S(1)}, u32[]{:S(2)}, u32[]{:S(2)}) %all-to-all-start.3) | async-done | bytes 1572896 | tf_op jit(solution)/shard_map/all_to_all | solution.py:104
  481.7 1.2 copy-done.4
  482.9 10.4 %fusion.11 = bf16[384,3584]{1,0:T(8,128)(2,1)S(1)} fusion(f32[384,3584]{1,0:T(8,128)} %divide_multiply_fusion, bf16[384,2048]{1,0:T(8,128)(2,1)} %bitcast.81, bf16[1,3584,2048]{2,1,0:T(8,128)(2,1)} %all-gather.5.cloned.1.call-done), kind=kOutput, calls=%fused_computation.10 | convolution fusion | flops 5639897088 | bytes 24510464 | tf_op jit(solution)/shard_map/dot_general | solution.py:16
  493.3 0.8 convolution_multiply_fusion.2
  494.1 0.6 copy-done.2
  494.7 1.4 fusion.20
  496.1 0.0 all-reduce.4.cloned.1.call-update
  496.1 0.0 all-reduce.6.cloned.1.call-start
  496.1 1.1 fusion.18
  497.3 0.7 constant_dynamic-slice_fusion
  498.0 92.3 %all-reduce.4.cloned.1.call-done = bf16[1,16,2048]{2,1,0:T(8,128)(2,1)} async-done(((bf16[1,16,2048]{2,1,0:T(8,128)(2,1)}), bf16[1,16,2048]{2,1,0:T(8,128)(2,1)}) %all-reduce.4.cloned.1.call-update) | async-done | bytes 65552 | tf_op jit(solution)/shard_map/psum | solution.py:122
  590.3 1.5 broadcast_in_dim.33
  591.9 84.2 %all-reduce.6.cloned.1.call-done = bf16[1,16,3584]{2,1,0:T(8,128)(2,1)} async-done(((bf16[1,16,3584]{2,1,0:T(8,128)(2,1)}), bf16[1,16,3584]{2,1,0:T(8,128)(2,1)}) %all-reduce.6.cloned.1.call-update) | async-done | bytes 114704 | tf_op jit(solution)/shard_map/psum | solution.py:123
  676.0 1.6 broadcast_in_dim.35
  (22 shorter events, 0.1 us)
Async XLA Ops:
  7.2 445.9 %copy-start = (bf16[2048,32]{0,1:T(8,128)(2,1)S(1)}, bf16[2048,32]{0,1:T(8,128)(2,1)}, u32[]{:S(2)}) copy-start(bf16[2048,32]{0,1:T(8,128)(2,1)} %param.19) | copy-start | bytes 393220
  7.2 308.4 %all-gather.3.cloned.1.call-start = ((), (), s32[]{:S(2)}) async-start(), calls=%async_computation.4 | async-start | bytes 15597568 | tf_op jit(solution)/shard_map/all_gather | solution.py:73
  7.9 391.0 %all-gather.5.cloned.1.call-start = ((), (), s32[]{:S(2)}) async-start(), calls=%async_computation.5 | async-start | bytes 15597568 | tf_op jit(solution)/shard_map/all_gather | solution.py:83
  8.7 32.0 %copy-start.5 = (bf16[1,128,3584]{2,1,0:T(8,128)(2,1)S(1)}, bf16[1,128,3584]{2,1,0:T(8,128)(2,1)}, u32[]{:S(2)}) copy-start(bf16[1,128,3584]{2,1,0:T(8,128)(2,1)} %param.15) | copy-start | bytes 2752516
  40.7 274.9 %copy-start.1 = (bf16[4,96,2048]{2,1,0:T(8,128)(2,1)}, bf16[4,96,2048]{2,1,0:T(8,128)(2,1)S(1)}, u32[]{:S(2)}) copy-start(bf16[4,96,2048]{2,1,0:T(8,128)(2,1)S(1)} %all_to_all.20) | copy-start | bytes 4718596
  47.2 7.2 %copy-start.7 = (bf16[1,16,2048]{2,1,0:T(8,128)(2,1)S(1)}, bf16[1,16,2048]{2,1,0:T(8,128)(2,1)}, u32[]{:S(2)}) copy-start(bf16[1,16,2048]{2,1,0:T(8,128)(2,1)} %param.17) | copy-start | bytes 196612
  47.2 256.9 %all-to-all-start.1 = ((bf16[16,1,128,3584]{3,2,1,0:T(8,128)(2,1)}), bf16[16,1,128,3584]{3,2,1,0:T(8,128)(2,1)}, u32[]{:S(2)}, u32[]{:S(2)}) async-start(bf16[16,1,128,3584]{3,2,1,0:T(8,128)(2,1)} %stack.2), calls=%async_computation.1 | async-start | bytes 29360128 | tf_op jit(solution)/shard_map/all_to_all | solution.py:8
  315.6 83.4 %copy-start.6 = (bf16[1,16,3584]{2,1,0:T(8,128)(2,1)S(1)}, bf16[1,16,3584]{2,1,0:T(8,128)(2,1)}, u32[]{:S(2)}) copy-start(bf16[1,16,3584]{2,1,0:T(8,128)(2,1)} %param.18) | copy-start | bytes 344068
  414.1 37.9 %copy-start.3 = (bf16[128,2048]{1,0:T(8,128)(2,1)S(1)}, bf16[128,2048]{1,0:T(8,128)(2,1)}, u32[]{:S(2)}) copy-start(bf16[128,2048]{1,0:T(8,128)(2,1)} %param.10) | copy-start | bytes 1572868
  426.5 26.8 %copy-start.8 = (s32[128]{0:T(128)S(1)}, s32[128]{0:T(128)}, u32[]{:S(2)}) copy-start(s32[128]{0:T(128)} %param.13) | copy-start | bytes 1540
  457.8 23.9 %all-to-all-start.3 = ((bf16[4,96,2048]{2,1,0:T(8,128)(2,1)}), bf16[4,96,2048]{2,1,0:T(8,128)(2,1)S(1)}, u32[]{:S(2)}, u32[]{:S(2)}) async-start(bf16[4,96,2048]{2,1,0:T(8,128)(2,1)} %bitcast.12), calls=%async_computation.3 | async-start | bytes 3145728 | tf_op jit(solution)/shard_map/all_to_all | solution.py:104
  461.4 129.0 %all-reduce.4.cloned.1.call-start = ((), (), s32[]{:S(2)}) async-start(), calls=%async_computation.6 | async-start | bytes 131072 | tf_op jit(solution)/shard_map/psum | solution.py:122
  481.7 1.2 copy-start.4
  493.3 1.4 copy-start.2
  496.1 179.9 %all-reduce.6.cloned.1.call-start = ((), (), s32[]{:S(2)}) async-start(), calls=%async_computation.7 | async-start | bytes 229376 | tf_op jit(solution)/shard_map/psum | solution.py:123
Sparse Core Ops, SparseCore 0:
  10.1 258.8 all-gather.2
  271.2 127.7 all-gather.4
  496.2 94.0 all-reduce.3
  594.0 81.9 all-reduce.5
